TPU v7x, 256 devices: a whole 4x4x8 slice. The times are simulated.
256 devices in a mesh: group: 4 (over z_hi, core), leaf: 64 (over y, z_lo, x).
Axes of the slice: x: 4, y: 4, z: 8 (z_hi: 2, z_lo: 4; z = z_hi * 4 + z_lo), core: 2. Of those that a mesh axis runs over, the one named last changes fastest.
Arguments:
- top_modes: bfloat16 [1024, 512], P('group'), may hold values from -6 to 6
- low_modes: bfloat16 [16384, 512], P(('group', 'leaf')), may hold values from -6 to 6
- anc_top: int32 [256, 8], P(('group', 'leaf')), may hold values from 0 to 15, all different within a row
- anc_low: int32 [256, 24], P(('group', 'leaf')), may hold values from 0 to 63, all different within a row
- coupling: bfloat16 [393216, 2048], P(('group', 'leaf')), may hold values from -0.125 to 0.125
- leaf_mass: bfloat16 [393216, 1536], P(('group', 'leaf')), may hold values from -0.15625 to 0.15625
- leaf_modes: bfloat16 [393216, 128], P(('group', 'leaf')), may hold values from -0.5 to 0.5
- leaf_coef: bfloat16 [32768, 512], P(('group', 'leaf')), may hold values from -6 to 6
- kinv_top: float32 [1024, 64], P('group'), may hold values from -0.0625 to 0.0625
- kinv_low: float32 [16384, 64], P(('group', 'leaf')), may hold values from -0.15625 to 0.15625
Outputs:
- new_top: float32 [1024, 512], P('group')
- new_low: float32 [16384, 512], P(('group', 'leaf'))
- leaf_proj: bfloat16 [32768, 512], P(('group', 'leaf'))
Inputs may be any that keep to these rules, and one draw needn't show every extreme that they name: `anc_top`: each row names 8 different top separator blocks. `anc_low`: each row names 24 different leaf indices of the leaf's own subtree.
All inputs are finite; a program needn't handle non-finite values.
Results may differ from a plain program's by a relative error of at most 0.0057.
Values may be sent and summed in bfloat16 or wider, within the bound.
A program may use at most 128 MiB of HBM per device.

v0:
```python
import jax
import jax.numpy as jnp
from jax import lax
from jax.sharding import PartitionSpec as P


def per_device(
    top_modes,
    low_modes,
    anc_top,
    anc_low,
    coupling,
    leaf_mass,
    leaf_modes,
    leaf_coef,
    kinv_top,
    kinv_low,
):
    sep_rows = kinv_low.shape[1]
    mode_count = low_modes.shape[1]
    top_slots = anc_top.shape[1]
    low_slots = anc_low.shape[1]
    owned_rows = kinv_top.shape[0]
    tops_all = lax.all_gather(top_modes, "group", axis=0, tiled=True)
    top_count = tops_all.shape[0] // sep_rows
    top_onehot = anc_top[0][:, None] == jnp.arange(top_count, dtype=jnp.int32)[None, :]
    top_sel = jnp.einsum(
        "ab,bsm->asm",
        top_onehot.astype(jnp.bfloat16),
        tops_all.reshape(top_count, sep_rows, mode_count),
        preferred_element_type=jnp.float32,
    )
    shard_rows = lax.all_gather(low_modes, "leaf", axis=0, tiled=True)
    block_count = shard_rows.shape[0] // sep_rows
    chosen = anc_low[0][:, None] == jnp.arange(block_count, dtype=jnp.int32)[None, :]
    low_sel = jnp.einsum(
        "ab,bsm->asm",
        chosen.astype(jnp.bfloat16),
        shard_rows.reshape(block_count, sep_rows, mode_count),
        preferred_element_type=jnp.float32,
    )
    stacked = (
        jnp.concatenate([top_sel, low_sel], axis=0).reshape(-1, mode_count).astype(jnp.bfloat16)
    )
    shapes = (
        jnp.dot(leaf_modes, leaf_coef, preferred_element_type=jnp.float32)
        - jnp.dot(coupling, stacked, preferred_element_type=jnp.float32)
    ).astype(jnp.bfloat16)
    weighted = jnp.dot(leaf_mass, shapes, preferred_element_type=jnp.float32).astype(jnp.bfloat16)
    loads = jnp.einsum("nk,nm->km", coupling, weighted, preferred_element_type=jnp.float32)
    leaf_proj = jnp.einsum(
        "nk,nm->km", leaf_modes, weighted, preferred_element_type=jnp.float32
    ).astype(jnp.bfloat16)
    top_part = loads[: top_slots * sep_rows].reshape(top_slots, sep_rows, mode_count)
    low_part = loads[top_slots * sep_rows :].reshape(low_slots, sep_rows, mode_count)
    top_term = jnp.einsum(
        "ab,asm->bsm", top_onehot.astype(jnp.float32), top_part, precision=lax.Precision.HIGHEST
    ).reshape(top_count * sep_rows, mode_count)
    summed = lax.psum(top_term, ("group", "leaf"))
    owned = lax.dynamic_slice_in_dim(summed, lax.axis_index("group") * owned_rows, owned_rows, 0)
    block_count = sep_rows * lax.axis_size("leaf") // sep_rows
    chosen = anc_low[0][:, None] == jnp.arange(block_count, dtype=jnp.int32)[None, :]
    low_loads = lax.psum_scatter(
        jnp.einsum(
            "ab,asm->bsm", chosen.astype(jnp.float32), low_part, precision=lax.Precision.HIGHEST
        ).reshape(sep_rows * lax.axis_size("leaf"), mode_count),
        "leaf",
        scatter_dimension=0,
        tiled=True,
    )
    new_top = jnp.einsum(
        "brs,bsm->brm",
        kinv_top.reshape(-1, sep_rows, sep_rows),
        owned.reshape(-1, sep_rows, mode_count),
        precision=lax.Precision.HIGHEST,
    ).reshape(owned_rows, mode_count)
    new_low = jnp.dot(kinv_low, low_loads, precision=lax.Precision.HIGHEST)
    return (new_top, new_low, leaf_proj)


def solution(mesh):
    return jax.shard_map(
        per_device,
        mesh=mesh,
        in_specs=(
            P("group", None),
            P(("group", "leaf"), None),
            P(("group", "leaf"), None),
            P(("group", "leaf"), None),
            P(("group", "leaf"), None),
            P(("group", "leaf"), None),
            P(("group", "leaf"), None),
            P(("group", "leaf"), None),
            P("group", None),
            P(("group", "leaf"), None),
        ),
        out_specs=(P("group", None), P(("group", "leaf"), None), P(("group", "leaf"), None)),
        check_vma=False,
    )
```

profile of v0, /device:TPU:6, one launch (start us, length us, event | category | flops | bytes accessed | tf_op | source)
XLA Modules:
  0.0 1079.3 jit_solution(7250876420761465487)
XLA Ops:
  8.0 0.7 all-gather.5.cloned.1.call-update
  8.7 35.7 %all-gather.3.cloned.1.call-done = bf16[1024,512]{1,0:T(8,128)(2,1)} async-done(((bf16[256,512]{1,0:T(8,128)(2,1)}), bf16[1024,512]{1,0:T(8,128)(2,1)}) %all-gather.3.cloned.1.call-update) | async-done | bytes 1048592 | tf_op jit(solution)/shard_map/all_gather | solution.py:24
  44.4 1.9 convolution_convert_fusion.1
  46.3 341.3 %all-gather.5.cloned.1.call-done = bf16[4096,512]{1,0:T(8,128)(2,1)} async-done(((bf16[64,512]{1,0:T(8,128)(2,1)}), bf16[4096,512]{1,0:T(8,128)(2,1)}) %all-gather.5.cloned.1.call-update) | async-done | bytes 4194320 | tf_op jit(solution)/shard_map/all_gather | solution.py:33
  387.7 6.9 fusion.5
  394.9 1.2 copy.19
  396.2 5.2 convolution_bitcast_fusion
  401.3 6.5 convolution_convert_fusion
  407.8 1.2 copy-done.2
  409.0 5.5 convolution_bitcast_fusion.1
  414.5 1.9 copy-done.1
  417.1 1.5 fusion.9
  418.6 2.5 copy.22
  421.3 1.8 slice-done
  423.1 2.4 copy.24
  425.5 7.4 fusion.2
  432.8 8.1 copy.26
  441.0 0.8 copy-done.4
  443.0 0.8 copy.27
  443.7 247.0 %all-reduce.2.cloned.1.call-done = f32[1024,512]{1,0:T(8,128)} async-done(((f32[1024,512]{1,0:T(8,128)}), f32[1024,512]{1,0:T(8,128)}) %all-reduce.2.cloned.1.call-update) | async-done | bytes 2097168 | tf_op jit(solution)/shard_map/psum | solution.py:59
  690.8 1.1 constant_dynamic-slice_fusion
  691.8 1.4 fusion.22
  693.2 377.7 %reduce-scatter.2.cloned.1.call-done = f32[64,512]{1,0:T(8,128)} async-done(((f32[4096,512]{1,0:T(8,128)}), f32[64,512]{1,0:T(8,128)}) %reduce-scatter.2.cloned.1.call-update) | async-done | bytes 131088 | tf_op jit(solution)/shard_map/reduce_scatter | solution.py:63
  1070.9 1.8 convolution_bitcast_fusion.2
  (33 shorter events, 3.1 us)
Async XLA Ops:
  7.2 394.2 %copy-start = (bf16[1536,128]{1,0:T(8,128)(2,1)S(1)}, bf16[1536,128]{1,0:T(8,128)(2,1)}, u32[]{:S(2)}) copy-start(bf16[1536,128]{1,0:T(8,128)(2,1)} %param.16) | copy-start | bytes 1179652
  7.2 37.2 %all-gather.3.cloned.1.call-start = ((), (), s32[]{:S(2)}) async-start(), calls=%async_computation.1 | async-start | bytes 1310720 | tf_op jit(solution)/shard_map/all_gather | solution.py:24
  7.9 379.8 %all-gather.5.cloned.1.call-start = ((), (), s32[]{:S(2)}) async-start(), calls=%async_computation.2 | async-start | bytes 4259840 | tf_op jit(solution)/shard_map/all_gather | solution.py:33
  8.7 682.1 %all-reduce.2.cloned.1.call-start = ((), (), s32[]{:S(2)}) async-start(), calls=%async_computation.3 | async-start | bytes 4194304 | tf_op jit(solution)/shard_map/psum | solution.py:59
  387.7 8.4 slice-start.1
  394.6 1.6 slice-start.2
  396.2 5.2 copy-start.8
  407.8 1.2 copy-start.2
  414.5 1.9 copy-start.1
  416.5 0.7 copy-start.7
  421.2 1.9 slice-start
  421.2 649.7 %reduce-scatter.2.cloned.1.call-start = ((), (), s32[]{:S(2)}) async-start(), calls=%async_computation.4 | async-start | bytes 8519680 | tf_op jit(solution)/shard_map/reduce_scatter | solution.py:63
  423.1 2.4 copy-start.6
  440.9 0.8 copy-start.4
  440.9 1.4 copy-start.3
  441.0 630.0 %copy-start.5 = (f32[64,64]{1,0:T(8,128)S(1)}, f32[64,64]{1,0:T(8,128)}, u32[]{:S(2)}) copy-start(f32[64,64]{1,0:T(8,128)} %param.19) | copy-start | bytes 49156
Sparse Core Ops, SparseCore 0:
  9.8 34.5 all-gather.2
  46.2 341.4 all-gather.4
  421.3 269.3 all-reduce.1
  693.2 377.7 reduce-scatter.1
where the time goes:
time: 1090 us; the launch traced here: 1080 us
  waiting for transfers between devices  1000 us (92%)
  matrix products  38.7 us (4%)
  local copies, waits for them, and re-layouts  23.1 us (2%)
  between operations  13.9 us (1%)
    reduce_scatter x1, waiting for transfers between devices, per_device(): lax.psum_scatter(jnp.einsum('ab,asm->bsm', chosen.astype(jnp.float32), lo...  378 us
    all_gather x1, waiting for transfers between devices, per_device(): shard_rows = lax.all_gather(low_modes, 'leaf', axis=0, tiled=True)  341 us
    psum x1, waiting for transfers between devices, per_device(): summed = lax.psum(top_term, ('group', 'leaf'))  247 us
    all_gather x1, waiting for transfers between devices, per_device(): tops_all = lax.all_gather(top_modes, 'group', axis=0, tiled=True)  35.7 us
  transfers between devices with their start and end apart: 4, of which 4 were waited for; matrix products, arithmetic and copies ran while one was open for 2% of the time, Pallas kernels for 0%

commit v1 on v0

v1 whole, which is shorter than its diff:
```python
import functools

import jax
import jax.numpy as jnp
from jax import lax
from jax.experimental import pallas as pl
from jax.experimental.pallas import tpu as pltpu
from jax.sharding import PartitionSpec as P

MESH = pl.DeviceIdType.MESH
F32 = jnp.float32
BF16 = jnp.bfloat16


class Comm:
    def __init__(self, send_sem, recv_sem):
        self.send_sem, self.recv_sem = send_sem, recv_sem
        self.count = 0
        self.sent = []

    def ids(self, amount):
        first = self.count
        self.count += amount
        return list(range(first, first + amount))

    def copy(self, m, src, dst, dev):
        return pltpu.make_async_remote_copy(
            src_ref=src,
            dst_ref=dst,
            send_sem=self.send_sem.at[m],
            recv_sem=self.recv_sem.at[m],
            device_id=dev,
            device_id_type=MESH,
        )

    def send(self, m, src, dst, dev):
        c = self.copy(m, src, dst, dev)
        c.start()
        self.sent.append(c)

    def recv(self, m, dst, dev):
        self.copy(m, dst, dst, dev).wait_recv()

    def finish(self):
        for c in self.sent:
            c.wait_send()


def gather_steps(comm, buf, own, q, p, z, qdev, pdev, zdev):
    mz = comm.ids(3)
    mp = comm.ids(4)
    mq = comm.ids(16)
    for d in (1, 2, 3):
        comm.send(mz[d - 1], own, buf.at[q, p, z], zdev((z + d) % 4))
    yield
    for d in (1, 2, 3):
        comm.recv(mz[d - 1], buf.at[q, p, (z + 4 - d) % 4], zdev((z + d) % 4))
    up, down, far = (p + 1) % 4, (p + 3) % 4, (p + 2) % 4
    qup, qdown, qfar = (q + 1) % 4, (q + 3) % 4, (q + 2) % 4

    def row(j, r):
        comm.send(mq[4 * j], buf.at[q, r], buf.at[q, r], qdev(qup))
        comm.send(mq[4 * j + 1], buf.at[q, r], buf.at[q, r], qdev(qdown))

    def pass_on(j, r):
        comm.recv(mq[4 * j], buf.at[qdown, r], qdev(qup))
        comm.send(mq[4 * j + 2], buf.at[qdown, r, pl.ds(0, 2)], buf.at[qdown, r, pl.ds(0, 2)], qdev(qup))
        comm.recv(mq[4 * j + 1], buf.at[qup, r], qdev(qdown))
        comm.send(mq[4 * j + 3], buf.at[qup, r, pl.ds(2, 2)], buf.at[qup, r, pl.ds(2, 2)], qdev(qdown))

    comm.send(mp[0], buf.at[q, p], buf.at[q, p], pdev(up))
    comm.send(mp[1], buf.at[q, p], buf.at[q, p], pdev(down))
    row(0, p)
    yield
    comm.recv(mp[0], buf.at[q, down], pdev(up))
    comm.send(mp[2], buf.at[q, down, pl.ds(0, 2)], buf.at[q, down, pl.ds(0, 2)], pdev(up))
    comm.recv(mp[1], buf.at[q, up], pdev(down))
    comm.send(mp[3], buf.at[q, up, pl.ds(2, 2)], buf.at[q, up, pl.ds(2, 2)], pdev(down))
    row(1, down)
    row(2, up)
    yield
    pass_on(0, p)
    yield
    comm.recv(mp[2], buf.at[q, far, pl.ds(0, 2)], pdev(up))
    comm.recv(mp[3], buf.at[q, far, pl.ds(2, 2)], pdev(down))
    row(3, far)
    yield
    pass_on(1, down)
    yield
    pass_on(2, up)
    yield
    pass_on(3, far)
    yield
    for j, r in enumerate((p, down, up, far)):
        comm.recv(mq[4 * j + 2], buf.at[qfar, r, pl.ds(0, 2)], qdev(qup))
        comm.recv(mq[4 * j + 3], buf.at[qfar, r, pl.ds(2, 2)], qdev(qdown))


def add_into(dst, *srcs):
    total = dst[...].astype(F32)
    for s in srcs:
        total = total + s[...].astype(F32)
    dst[...] = total.astype(dst.dtype)


def scatter_steps(comm, s, r1a, r1b, r2a, r2b, rp1, rp2a, rp2b, rz, out, q, p, z, qdev, pdev, zdev):
    m1 = comm.ids(8)
    m2 = comm.ids(8)
    mp1 = comm.ids(2)
    mp2 = comm.ids(2)
    mz = comm.ids(3)
    up, down, far = (p + 1) % 4, (p + 3) % 4, (p + 2) % 4
    qup, qdown, qfar = (q + 1) % 4, (q + 3) % 4, (q + 2) % 4
    lo, hi = pl.ds(0, 2), pl.ds(2, 2)
    order = (far, up, down, p)
    for j, r in enumerate(order):
        comm.send(m1[2 * j], s.at[qfar, r, lo], r1a.at[r], qdev(qup))
        comm.send(m1[2 * j + 1], s.at[qfar, r, hi], r1b.at[r], qdev(qdown))
    yield
    for j, r in enumerate(order):
        comm.recv(m1[2 * j], r1a.at[r], qdev(qup))
        add_into(s.at[qup, r, lo], r1a.at[r])
        comm.send(m2[2 * j], s.at[qup, r], r2a.at[r], qdev(qup))
        comm.recv(m1[2 * j + 1], r1b.at[r], qdev(qdown))
        add_into(s.at[qdown, r, hi], r1b.at[r])
        comm.send(m2[2 * j + 1], s.at[qdown, r], r2b.at[r], qdev(qdown))
        yield
    for j, r in enumerate(order):
        comm.recv(m2[2 * j], r2a.at[r], qdev(qup))
        comm.recv(m2[2 * j + 1], r2b.at[r], qdev(qdown))
        add_into(s.at[q, r], r2a.at[r], r2b.at[r])
        if j == 0:
            comm.send(mp1[0], s.at[q, far, lo], rp1.at[0], pdev(up))
            comm.send(mp1[1], s.at[q, far, hi], rp1.at[1], pdev(down))
        if j == 1:
            comm.recv(mp1[0], rp1.at[0], pdev(up))
            add_into(s.at[q, up, lo], rp1.at[0])
            comm.send(mp2[0], s.at[q, up], rp2a, pdev(up))
        if j == 2:
            comm.recv(mp1[1], rp1.at[1], pdev(down))
            add_into(s.at[q, down, hi], rp1.at[1])
            comm.send(mp2[1], s.at[q, down], rp2b, pdev(down))
        yield
    comm.recv(mp2[0], rp2a, pdev(up))
    comm.recv(mp2[1], rp2b, pdev(down))
    add_into(s.at[q, p], rp2a, rp2b)
    for d in (1, 2, 3):
        comm.send(mz[d - 1], s.at[q, p, (z + d) % 4], rz.at[d - 1], zdev((z + d) % 4))
    yield
    for d in (1, 2, 3):
        comm.recv(mz[d - 1], rz.at[d - 1], zdev((z + d) % 4))
    total = s[q, p, z].astype(F32)
    for d in range(3):
        total = total + rz[d].astype(F32)
    out[...] = total


def run_together(*steps):
    live = list(steps)
    while live:
        for g in list(live):
            try:
                next(g)
            except StopIteration:
                live.remove(g)


def kernel(
    anc_top, anc_low, inv_top, inv_low,
    top_in, low_in, coef, kinv_top, kinv_low,
    coupling_hbm, mass_hbm, modes_hbm,
    new_top, new_low, proj,
    coupling, mass, modes, turned,
    low_a, low_b, tops, stacked, shapes, weighted,
    loads, top_loads, give, take,
    s_a, s_b, r1, r2, rp1, rp2, rz, sums,
    far_tile, gath_a, gath_b, full_top, full_low,
    local_sem, send_sem, recv_sem,
):
    leaf = lax.axis_index("leaf")
    group = lax.axis_index("group")
    y, z, x = leaf // 16, (leaf // 4) % 4, leaf % 4
    half, core = group // 2, group % 2
    mate = half * 2 + 1 - core
    across = (group + 2) % 4
    mate_across = (mate + 2) % 4

    def xdev(v):
        return {"leaf": y * 16 + z * 4 + v}

    def ydev(v):
        return {"leaf": v * 16 + z * 4 + x}

    def zdev(v):
        return {"leaf": y * 16 + v * 4 + x}

    mate_dev, across_dev = {"group": mate}, {"group": across}

    loading = [
        pltpu.make_async_copy(src, dst, local_sem.at[i])
        for i, (src, dst) in enumerate(((coupling_hbm, coupling), (modes_hbm, modes), (mass_hbm, mass)))
    ]
    for c in loading:
        c.start()

    barrier = pltpu.get_barrier_semaphore()
    peers = [xdev((x + d) % 4) for d in (1, 2, 3)] + [ydev((y + 1) % 4), ydev((y + 3) % 4)]
    peers += [zdev((z + d) % 4) for d in (1, 2, 3)] + [mate_dev, across_dev]
    for dev in peers:
        pl.semaphore_signal(barrier, inc=1, device_id=dev, device_id_type=MESH)
    low_a[x, y, z] = low_in[0]
    low_b[y, x, z] = low_in[1]
    tops[group] = top_in[...]
    pl.semaphore_wait(barrier, len(peers))

    comm = Comm(send_sem, recv_sem)
    steps_a = gather_steps(comm, low_a, low_in.at[0], x, y, z, xdev, ydev, zdev)
    steps_b = gather_steps(comm, low_b, low_in.at[1], y, x, z, ydev, xdev, zdev)
    next(steps_a)
    next(steps_b)

    mt = comm.ids(9)
    comm.send(mt[0], top_in, tops.at[group], mate_dev)
    comm.send(mt[1], top_in.at[x], tops.at[group, x], across_dev)

    def turn(i):
        @pl.loop(0, 8)
        def _(k):
            cols = pl.ds(pl.multiple_of(k * 256, 256), 256)
            turned[cols, pl.ds(i * 256, 256)] = coupling[pl.ds(i * 256, 256), cols].T

    def turn_modes():
        for i in range(6):
            turned[pl.ds(2048, 128), pl.ds(i * 256, 256)] = modes[pl.ds(i * 256, 256), :].T

    next(steps_a)
    next(steps_b)
    loading[0].wait()
    turn(0)
    next(steps_a)
    next(steps_b)
    turn(1)
    comm.recv(mt[1], tops.at[across, x], across_dev)
    for d in (1, 2, 3):
        comm.send(mt[1 + d], tops.at[across, x], tops.at[across, x], xdev((x + d) % 4))
    comm.send(mt[5], tops.at[across, x], tops.at[across, x], mate_dev)
    next(steps_a)
    next(steps_b)
    turn(2)
    next(steps_a)
    next(steps_b)
    turn(3)
    for d in (1, 2, 3):
        got = tops.at[across, (x + 4 - d) % 4]
        comm.recv(mt[1 + d], got, xdev((x + d) % 4))
        comm.send(mt[5 + d], got, got, mate_dev)
    next(steps_a)
    next(steps_b)
    turn(4)
    next(steps_a)
    next(steps_b)
    turn(5)
    loading[1].wait()
    turn_modes()
    next(steps_a)
    next(steps_b)
    comm.recv(mt[0], tops.at[mate], mate_dev)
    comm.recv(mt[5], tops.at[mate_across, x], mate_dev)
    for d in (1, 2, 3):
        comm.recv(mt[5 + d], tops.at[mate_across, (x + 4 - d) % 4], mate_dev)
    loading[2].wait()
    run_together(steps_a, steps_b)

    for j in range(8):
        b = anc_top[j]
        stacked[pl.ds(j * 64, 64), :] = tops[b // 4, b % 4]
    for j in range(24):
        k = anc_low[j]
        ky, kz, kx = k // 16, (k // 4) % 4, k % 4
        stacked[pl.ds(512 + j * 64, 32), :] = low_a[kx, ky, kz]
        stacked[pl.ds(512 + j * 64 + 32, 32), :] = low_b[ky, kx, kz]

    @pl.loop(0, 6)
    def _(i):
        rows = pl.ds(pl.multiple_of(i * 256, 256), 256)
        got = jnp.dot(modes[rows, :], coef[...], preferred_element_type=F32)
        got = got - jnp.dot(coupling[rows, :], stacked[...], preferred_element_type=F32)
        shapes[rows, :] = got.astype(BF16)

    @pl.loop(0, 6)
    def _(i):
        rows = pl.ds(pl.multiple_of(i * 256, 256), 256)
        weighted[rows, :] = jnp.dot(mass[rows, :], shapes[...], preferred_element_type=F32).astype(BF16)

    top_loads[0] = jnp.zeros(top_loads.shape[1:], BF16)
    loads[0] = jnp.zeros(loads.shape[1:], BF16)

    @pl.loop(0, 2)
    def _(i):
        rows = pl.ds(pl.multiple_of(i * 256, 256), 256)
        got = jnp.dot(turned[rows, :], weighted[...], preferred_element_type=F32).astype(BF16)
        for b in range(4):
            for r in range(4):
                for c in range(4):
                    top_loads[1 + i * 4 + b, r, c] = got[b * 64 + r * 16 : b * 64 + r * 16 + 16, c * 128 : c * 128 + 128]

    @pl.loop(0, 64)
    def _(t):
        b, r, c = t // 16, (t // 4) % 4, t % 4
        give[0, t] = top_loads[inv_top[4 * (1 - core) + b], r, c]
        give[1, t] = top_loads[inv_top[8 + 4 * (1 - core) + b], r, c]

    mx = comm.ids(2)
    comm.send(mx[0], give, take, mate_dev)

    @pl.loop(0, 6)
    def _(i):
        rows = pl.ds(pl.multiple_of(512 + i * 256, 256), 256)
        got = jnp.dot(turned[rows, :], weighted[...], preferred_element_type=F32).astype(BF16)
        for b in range(4):
            for r in range(4):
                for c in range(4):
                    loads[1 + i * 4 + b, r // 2, (r % 2) * 4 + c] = got[
                        b * 64 + r * 16 : b * 64 + r * 16 + 16, c * 128 : c * 128 + 128
                    ]

    comm.recv(mx[0], take, mate_dev)

    @pl.loop(0, 64)
    def _(t):
        a, b, c = t // 16, (t // 4) % 4, t % 4
        j = inv_low[b * 16 + c * 4 + a]
        s_a[a, b, c, pl.ds(0, 8)] = loads[j, 0]
        s_b[b, a, c, pl.ds(0, 8)] = loads[j, 1]
        mine = top_loads[inv_top[4 * core + a], b, c].astype(F32)
        s_a[a, b, c, 8] = (mine + take[0, t].astype(F32)).astype(BF16)
        mine = top_loads[inv_top[8 + 4 * core + a], b, c].astype(F32)
        s_b[b, a, c, 8] = (mine + take[1, t].astype(F32)).astype(BF16)

    sc_a = scatter_steps(
        comm, s_a, r1.at[0, 0], r1.at[0, 1], r2.at[0, 0], r2.at[0, 1], rp1.at[0], rp2.at[0, 0], rp2.at[0, 1],
        rz.at[0], sums.at[0], x, y, z, xdev, ydev, zdev,
    )
    sc_b = scatter_steps(
        comm, s_b, r1.at[1, 0], r1.at[1, 1], r2.at[1, 0], r2.at[1, 1], rp1.at[1], rp2.at[1, 0], rp2.at[1, 1],
        rz.at[1], sums.at[1], y, x, z, ydev, xdev, zdev,
    )
    next(sc_a)
    next(sc_b)
    proj[...] = jnp.dot(turned[pl.ds(2048, 128), :], weighted[...], preferred_element_type=F32).astype(BF16)
    run_together(sc_a, sc_b)

    comm.send(mx[1], sums.at[1 - half, 8], far_tile, across_dev)
    for h in range(2):
        for r in range(2):
            for c in range(4):
                full_low[h * 32 + r * 16 : h * 32 + r * 16 + 16, c * 128 : c * 128 + 128] = sums[h, r * 4 + c]
    new_low[...] = jnp.dot(kinv_low[...], full_low[...], preferred_element_type=F32, precision=lax.Precision.HIGHEST)
    comm.recv(mx[1], far_tile, across_dev)
    tile = sums[half, 8] + far_tile[...]
    gath_a[x, y, z] = tile[0:8, :]
    gath_b[y, x, z] = tile[8:16, :]
    run_together(
        gather_steps(comm, gath_a, gath_a.at[x, y, z], x, y, z, xdev, ydev, zdev),
        gather_steps(comm, gath_b, gath_b.at[y, x, z], y, x, z, ydev, xdev, zdev),
    )
    for b in range(4):
        for r in range(4):
            for c in range(4):
                cols = pl.ds(c * 128, 128)
                full_top[b, pl.ds(r * 16, 8), cols] = gath_a[b, r, c]
                full_top[b, pl.ds(r * 16 + 8, 8), cols] = gath_b[r, b, c]
    for b in range(4):
        rows = pl.ds(b * 64, 64)
        new_top[rows, :] = jnp.dot(
            kinv_top[rows, :], full_top[b], preferred_element_type=F32, precision=lax.Precision.HIGHEST
        )
    comm.finish()


def per_device(top_modes, low_modes, anc_top, anc_low, coupling, leaf_mass, leaf_modes, leaf_coef, kinv_top, kinv_low):
    inv_top = jnp.sum(
        jnp.where(anc_top == jnp.arange(16, dtype=jnp.int32)[:, None], jnp.arange(1, 9, dtype=jnp.int32)[None, :], 0), axis=1
    )
    inv_low = jnp.sum(
        jnp.where(anc_low == jnp.arange(64, dtype=jnp.int32)[:, None], jnp.arange(1, 25, dtype=jnp.int32)[None, :], 0), axis=1
    )
    smem = pl.BlockSpec(memory_space=pltpu.SMEM)
    vmem = pl.BlockSpec(memory_space=pltpu.VMEM)
    hbm = pl.BlockSpec(memory_space=pl.ANY)
    piece = (16, 128)
    messages = 46 + 9 + 2 + 46 + 46
    return pl.pallas_call(
        kernel,
        out_shape=(
            jax.ShapeDtypeStruct((256, 512), F32),
            jax.ShapeDtypeStruct((64, 512), F32),
            jax.ShapeDtypeStruct((128, 512), BF16),
        ),
        in_specs=[smem] * 4 + [vmem] * 5 + [hbm] * 3,
        out_specs=(vmem, vmem, vmem),
        scratch_shapes=[
            pltpu.VMEM((1536, 2048), BF16),
            pltpu.VMEM((1536, 1536), BF16),
            pltpu.VMEM((1536, 128), BF16),
            pltpu.VMEM((2176, 1536), BF16),
            pltpu.VMEM((4, 4, 4, 32, 512), BF16),
            pltpu.VMEM((4, 4, 4, 32, 512), BF16),
            pltpu.VMEM((4, 4, 64, 512), BF16),
            pltpu.VMEM((2048, 512), BF16),
            pltpu.VMEM((1536, 512), BF16),
            pltpu.VMEM((1536, 512), BF16),
            pltpu.VMEM((25, 2, 8) + piece, BF16),
            pltpu.VMEM((9, 4, 4) + piece, BF16),
            pltpu.VMEM((2, 64) + piece, BF16),
            pltpu.VMEM((2, 64) + piece, BF16),
            pltpu.VMEM((4, 4, 4, 9) + piece, BF16),
            pltpu.VMEM((4, 4, 4, 9) + piece, BF16),
            pltpu.VMEM((2, 2, 4, 2, 9) + piece, BF16),
            pltpu.VMEM((2, 2, 4, 4, 9) + piece, BF16),
            pltpu.VMEM((2, 2, 2, 9) + piece, BF16),
            pltpu.VMEM((2, 2, 4, 9) + piece, BF16),
            pltpu.VMEM((2, 3, 9) + piece, BF16),
            pltpu.VMEM((2, 9) + piece, F32),
            pltpu.VMEM(piece, F32),
            pltpu.VMEM((4, 4, 4, 8, 128), F32),
            pltpu.VMEM((4, 4, 4, 8, 128), F32),
            pltpu.VMEM((4, 64, 512), F32),
            pltpu.VMEM((64, 512), F32),
            pltpu.SemaphoreType.DMA((3,)),
            pltpu.SemaphoreType.DMA((messages,)),
            pltpu.SemaphoreType.DMA((messages,)),
        ],
        compiler_params=pltpu.CompilerParams(
            collective_id=0, has_side_effects=True, vmem_limit_bytes=63000 * 1024
        ),
    )(
        anc_top[0], anc_low[0], inv_top, inv_low,
        top_modes.reshape(4, 64, 512), low_modes.reshape(2, 32, 512), leaf_coef, kinv_top, kinv_low,
        coupling, leaf_mass, leaf_modes,
    )


def solution(mesh):
    both = P(("group", "leaf"), None)
    return jax.shard_map(
        per_device,
        mesh=mesh,
        in_specs=(P("group", None), both, both, both, both, both, both, both, P("group", None), both),
        out_specs=(P("group", None), both, both),
        check_vma=False,
    )
```

time: 1090 us -> 129 us (0.12)
  waiting for transfers between devices: 1000 us -> 0 us
  Pallas kernels: 0 us -> 119 us
  matrix products: 38.7 us -> 0 us
  local copies, waits for them, and re-layouts: 23.1 us -> 6.6 us
  between operations: 13.9 us -> 0.65 us
    reduce_scatter x1 -> x0, waiting for transfers between devices: 378 us -> none  [per_device(): lax.psum_scatter(jnp.einsum('ab,asm->bsm', chosen.astype(jnp.float32), lo...]
    all_gather x2 -> x0, waiting for transfers between devices: 377 us -> none  [the longest x1 341 us: per_device(): shard_rows = lax.all_gather(low_modes, 'leaf', axis=0, tiled=True)]
    psum x1 -> x0, waiting for transfers between devices: 247 us -> none  [per_device(): summed = lax.psum(top_term, ('group', 'leaf'))]
    pallas_call x0 -> x1, Pallas kernels: none -> 119 us  [per_device(): pl.pallas_call(kernel, out_shape=(jax.ShapeDtypeStruct((256, 512), F32),...]
    dot_general x10 -> x0, matrix products: 38.7 us -> none  [the longest x1 7.38 us: per_device(): jnp.einsum('ab,asm->bsm', chosen.astype(jnp.float32), low_part, precision...]
  transfers between devices with their start and end apart: 4 -> 0, of which waited for: 4 -> 0; matrix products, arithmetic and copies ran while one was open for 2% -> 0% of each run, Pallas kernels for 0% -> 0%
where the time goes in v1:
time: 129 us
  Pallas kernels  119 us (92%)
  local copies, waits for them, and re-layouts  6.6 us (5%)
  other arithmetic  2.51 us (2%)
    pallas_call x1, Pallas kernels, per_device(): pl.pallas_call(kernel, out_shape=(jax.ShapeDtypeStruct((256, 512), F32),...  119 us
    unnamed x4, local copies, waits for them, and re-layouts  6.6 us

profile of v1, /device:TPU:6, one launch (start us, length us, event | category | flops | bytes accessed | tf_op | source)
XLA Modules:
  0.0 128.6 jit_solution(3391364840975936878)
XLA Ops:
  0.6 1.3 select_reduce_fusion.1.inv_top
  1.9 1.3 select_reduce_fusion.inv_low
  3.1 1.6 %copy.14.kinv_top = f32[256,64]{1,0:T(8,128)} copy(f32[256,64]{0,1:T(8,128)} %param.18) | data formatting | bytes 131072 | tf_op args[8]
  4.7 118.9 %shard_map.121 = (f32[256,512]{1,0:T(8,128)}, f32[64,512]{1,0:T(8,128)}, bf16[128,512]{1,0:T(8,128)(2,1)}) custom-call(s32[8]{0:T(128)} %bitcast.7, s32[24]{0:T(128)} %bitcast.9, s32[16]{0:T(128)} %select_reduce_fusion.1.inv_top, s32[64]{0:T(128)} %select_reduce_fusion.inv_low, bf16[4,64,512]{2,1,0:T(8,128)(2,1)} %bitcast.4, bf16[2,32,512]{2,1,0:T(8,128)(2,1)} %bitcast.5, ...), custom_call_target="tpu_custom_call" | custom-call | tf_op jit(solution)/shard_map/pallas_call | solution.py:393
  123.6 1.9 %copy.18 = f32[256,512]{1,0:T(8,128)} copy(f32[256,512]{1,0:T(8,128)} %get-tuple-element.6) | data formatting | bytes 1048576
  125.5 1.6 %copy.19 = f32[64,512]{1,0:T(8,128)} copy(f32[64,512]{1,0:T(8,128)} %get-tuple-element.7) | data formatting | bytes 262144
  127.0 1.6 %copy.20 = bf16[128,512]{1,0:T(8,128)(2,1)} copy(bf16[128,512]{1,0:T(8,128)(2,1)} %get-tuple-element.8) | data formatting | bytes 262144
  (2 shorter events, 0.0 us)

commit v2 on v1

v2 whole, which is shorter than its diff:
```python
import functools

import jax
import jax.numpy as jnp
from jax import lax
from jax.experimental import pallas as pl
from jax.experimental.pallas import tpu as pltpu
from jax.sharding import PartitionSpec as P

MESH = pl.DeviceIdType.MESH
F32 = jnp.float32
BF16 = jnp.bfloat16


GATHER_PLAN = "af0at1a2ta3bat4abt5abt6ab"
FIRST_PLAN = "vbvbvbvbvvvsj"
SECOND_PLAN = "wwsssswwwsqwsssu"
LAST_PLAN = "kpsuuuuqspuuqpuuuqpu"


class Comm:
    def __init__(self, send_sem, recv_sem):
        self.send_sem, self.recv_sem = send_sem, recv_sem
        self.count = 0
        self.sent = []

    def ids(self, amount):
        first = self.count
        self.count += amount
        return list(range(first, first + amount))

    def copy(self, m, src, dst, dev):
        return pltpu.make_async_remote_copy(
            src_ref=src,
            dst_ref=dst,
            send_sem=self.send_sem.at[m],
            recv_sem=self.recv_sem.at[m],
            device_id=dev,
            device_id_type=MESH,
        )

    def send(self, m, src, dst, dev):
        c = self.copy(m, src, dst, dev)
        c.start()
        self.sent.append(c)

    def recv(self, m, dst, dev):
        self.copy(m, dst, dst, dev).wait_recv()

    def finish(self):
        for c in self.sent:
            c.wait_send()


def gather_steps(comm, buf, own, q, p, z, qdev, pdev, zdev):
    mz = comm.ids(3)
    mp = comm.ids(4)
    mq = comm.ids(16)
    for d in (1, 2, 3):
        comm.send(mz[d - 1], own, buf.at[q, p, z], zdev((z + d) % 4))
    yield
    for d in (1, 2, 3):
        comm.recv(mz[d - 1], buf.at[q, p, (z + 4 - d) % 4], zdev((z + d) % 4))
    up, down, far = (p + 1) % 4, (p + 3) % 4, (p + 2) % 4
    qup, qdown, qfar = (q + 1) % 4, (q + 3) % 4, (q + 2) % 4

    def row(j, r):
        comm.send(mq[4 * j], buf.at[q, r], buf.at[q, r], qdev(qup))
        comm.send(mq[4 * j + 1], buf.at[q, r], buf.at[q, r], qdev(qdown))

    def pass_on(j, r):
        comm.recv(mq[4 * j], buf.at[qdown, r], qdev(qup))
        comm.send(mq[4 * j + 2], buf.at[qdown, r, pl.ds(0, 2)], buf.at[qdown, r, pl.ds(0, 2)], qdev(qup))
        comm.recv(mq[4 * j + 1], buf.at[qup, r], qdev(qdown))
        comm.send(mq[4 * j + 3], buf.at[qup, r, pl.ds(2, 2)], buf.at[qup, r, pl.ds(2, 2)], qdev(qdown))

    comm.send(mp[0], buf.at[q, p], buf.at[q, p], pdev(up))
    comm.send(mp[1], buf.at[q, p], buf.at[q, p], pdev(down))
    row(0, p)
    yield
    comm.recv(mp[0], buf.at[q, down], pdev(up))
    comm.send(mp[2], buf.at[q, down, pl.ds(0, 2)], buf.at[q, down, pl.ds(0, 2)], pdev(up))
    comm.recv(mp[1], buf.at[q, up], pdev(down))
    comm.send(mp[3], buf.at[q, up, pl.ds(2, 2)], buf.at[q, up, pl.ds(2, 2)], pdev(down))
    row(1, down)
    row(2, up)
    yield
    pass_on(0, p)
    yield
    comm.recv(mp[2], buf.at[q, far, pl.ds(0, 2)], pdev(up))
    comm.recv(mp[3], buf.at[q, far, pl.ds(2, 2)], pdev(down))
    row(3, far)
    yield
    pass_on(1, down)
    yield
    pass_on(2, up)
    yield
    pass_on(3, far)
    yield
    for j, r in enumerate((p, down, up, far)):
        comm.recv(mq[4 * j + 2], buf.at[qfar, r, pl.ds(0, 2)], qdev(qup))
        comm.recv(mq[4 * j + 3], buf.at[qfar, r, pl.ds(2, 2)], qdev(qdown))


def add_into(dst, *srcs):
    total = dst[...].astype(F32)
    for s in srcs:
        total = total + s[...].astype(F32)
    dst[...] = total.astype(dst.dtype)


def scatter_steps(comm, s, r1, r2, rp1, rp2, rz, out, q, p, z, qdev, pdev, zdev):
    m1 = comm.ids(8)
    m2 = comm.ids(8)
    mp1 = comm.ids(2)
    mp2 = comm.ids(2)
    mz = comm.ids(3)
    up, down, far = (p + 1) % 4, (p + 3) % 4, (p + 2) % 4
    qup, qdown, qfar = (q + 1) % 4, (q + 3) % 4, (q + 2) % 4
    lo, hi = pl.ds(0, 2), pl.ds(2, 2)
    order = (far, up, down, p)
    for j, r in enumerate(order):
        comm.send(m1[2 * j], s.at[qfar, r, lo], r1.at[0, r], qdev(qup))
        comm.send(m1[2 * j + 1], s.at[qfar, r, hi], r1.at[1, r], qdev(qdown))
    yield
    for j, r in enumerate(order):
        comm.recv(m1[2 * j], r1.at[0, r], qdev(qup))
        add_into(s.at[qup, r, lo], r1.at[0, r])
        comm.send(m2[2 * j], s.at[qup, r], r2.at[0, r], qdev(qup))
        comm.recv(m1[2 * j + 1], r1.at[1, r], qdev(qdown))
        add_into(s.at[qdown, r, hi], r1.at[1, r])
        comm.send(m2[2 * j + 1], s.at[qdown, r], r2.at[1, r], qdev(qdown))
        yield
    for j, r in enumerate(order):
        comm.recv(m2[2 * j], r2.at[0, r], qdev(qup))
        comm.recv(m2[2 * j + 1], r2.at[1, r], qdev(qdown))
        add_into(s.at[q, r], r2.at[0, r], r2.at[1, r])
        if j == 0:
            comm.send(mp1[0], s.at[q, far, lo], rp1.at[0], pdev(up))
            comm.send(mp1[1], s.at[q, far, hi], rp1.at[1], pdev(down))
        if j == 1:
            comm.recv(mp1[0], rp1.at[0], pdev(up))
            add_into(s.at[q, up, lo], rp1.at[0])
            comm.send(mp2[0], s.at[q, up], rp2.at[0], pdev(up))
        if j == 2:
            comm.recv(mp1[1], rp1.at[1], pdev(down))
            add_into(s.at[q, down, hi], rp1.at[1])
            comm.send(mp2[1], s.at[q, down], rp2.at[1], pdev(down))
        yield
    comm.recv(mp2[0], rp2.at[0], pdev(up))
    comm.recv(mp2[1], rp2.at[1], pdev(down))
    add_into(s.at[q, p], rp2.at[0], rp2.at[1])
    for d in (1, 2, 3):
        comm.send(mz[d - 1], s.at[q, p, (z + d) % 4], rz.at[d - 1], zdev((z + d) % 4))
    yield
    for d in (1, 2, 3):
        comm.recv(mz[d - 1], rz.at[d - 1], zdev((z + d) % 4))
    total = s[q, p, z].astype(F32)
    for d in range(3):
        total = total + rz[d].astype(F32)
    out[...] = total


def top_steps(comm, tops, group, mate, across, mate_across, x, y, z, xdev, ydev, zdev, mate_dev, across_dev):
    m_own = comm.ids(1)
    m_far = comm.ids(2)
    m_line = comm.ids(6)
    m_ring = comm.ids(8)
    m_mate = comm.ids(8)
    lines = ((0, x, xdev), (1, y, ydev))
    lo, hi = pl.ds(0, 2), pl.ds(2, 2)
    for h, v, _ in lines:
        got = tops.at[group, v, h, z]
        comm.send(m_far[h], got, got, across_dev)
    comm.send(m_own[0], tops.at[group], tops.at[group], mate_dev)
    yield
    for h, v, _ in lines:
        got = tops.at[across, v, h, z]
        comm.recv(m_far[h], got, across_dev)
        for d in (1, 2, 3):
            comm.send(m_line[3 * h + d - 1], got, got, zdev((z + d) % 4))
    yield
    for h, v, dev in lines:
        for d in (1, 2, 3):
            comm.recv(m_line[3 * h + d - 1], tops.at[across, v, h, (z + 4 - d) % 4], zdev((z + d) % 4))
        got = tops.at[across, v, h]
        comm.send(m_ring[4 * h], got, got, dev((v + 1) % 4))
        comm.send(m_ring[4 * h + 1], got, got, dev((v + 3) % 4))
        comm.send(m_mate[4 * h], got, got, mate_dev)
    yield
    for h, v, dev in lines:
        low, high = tops.at[across, (v + 3) % 4, h], tops.at[across, (v + 1) % 4, h]
        comm.recv(m_ring[4 * h], low, dev((v + 1) % 4))
        comm.send(m_ring[4 * h + 2], low.at[lo], low.at[lo], dev((v + 1) % 4))
        comm.send(m_mate[4 * h + 1], low, low, mate_dev)
        comm.recv(m_ring[4 * h + 1], high, dev((v + 3) % 4))
        comm.send(m_ring[4 * h + 3], high.at[hi], high.at[hi], dev((v + 3) % 4))
        comm.send(m_mate[4 * h + 2], high, high, mate_dev)
    yield
    for h, v, dev in lines:
        got = tops.at[across, (v + 2) % 4, h]
        comm.recv(m_ring[4 * h + 2], got.at[lo], dev((v + 1) % 4))
        comm.recv(m_ring[4 * h + 3], got.at[hi], dev((v + 3) % 4))
        comm.send(m_mate[4 * h + 3], got, got, mate_dev)
    yield
    comm.recv(m_own[0], tops.at[mate], mate_dev)
    for h, v, _ in lines:
        for i, w in enumerate((v, (v + 3) % 4, (v + 1) % 4, (v + 2) % 4)):
            comm.recv(m_mate[4 * h + i], tops.at[mate_across, w, h], mate_dev)


def advance(*steps):
    for g in steps:
        next(g, None)


def run_together(*steps):
    live = list(steps)
    while live:
        for g in list(live):
            try:
                next(g)
            except StopIteration:
                live.remove(g)


def kernel(
    anc_top, anc_low,
    top_hbm, low_hbm, coef_hbm, kinv_top_hbm, kinv_low_hbm, coupling_hbm, mass_hbm, modes_hbm,
    new_top, new_low, proj,
    coef, kinv_top, kinv_low, coupling, mass, modes, turned, kinv_turned,
    low_a0, low_a1, low_b0, low_b1, tops, stacked, shapes, weighted,
    loads, top_loads, give, take,
    s_low, r1, r2, rp1, rp2, rz, sums,
    s_top, tp, line_out, line_in, gath, full_top, full_low,
    inv_top, inv_low, local_sem, send_sem, recv_sem,
):
    low_a, low_b = (low_a0, low_a1), (low_b0, low_b1)
    leaf = lax.axis_index("leaf")
    group = lax.axis_index("group")
    y, z, x = leaf // 16, (leaf // 4) % 4, leaf % 4
    half, core = group // 2, group % 2
    mate = half * 2 + 1 - core
    across = (group + 2) % 4
    mate_across = (mate + 2) % 4

    def xdev(v):
        return {"leaf": y * 16 + z * 4 + v}

    def ydev(v):
        return {"leaf": v * 16 + z * 4 + x}

    def zdev(v):
        return {"leaf": y * 16 + v * 4 + x}

    def far_zdev(v):
        return {"group": across, "leaf": y * 16 + v * 4 + x}

    mate_dev, across_dev = {"group": mate}, {"group": across}
    lines = ((x, y, z, xdev, ydev, zdev), (y, x, z, ydev, xdev, zdev))

    barrier = pltpu.get_barrier_semaphore()
    peers = [
        {"leaf": (y + b) % 4 * 16 + z * 4 + (x + a) % 4} for a in range(4) for b in range(4) if a + b > 0
    ]
    peers += [zdev((z + d) % 4) for d in (1, 2, 3)] + [mate_dev] + [far_zdev((z + d) % 4) for d in range(4)]
    for dev in peers:
        pl.semaphore_signal(barrier, inc=1, device_id=dev, device_id_type=MESH)

    fetched = [
        (low_hbm.at[0, :, pl.ds(0, 256)], low_a[0].at[x, y, z]),
        (low_hbm.at[1, :, pl.ds(0, 256)], low_b[0].at[y, x, z]),
        (low_hbm.at[0, :, pl.ds(256, 256)], low_a[1].at[x, y, z]),
        (low_hbm.at[1, :, pl.ds(256, 256)], low_b[1].at[y, x, z]),
        *((top_hbm.at[:, :, :, pl.ds(128 * k, 128)], tops.at[group, :, :, k]) for k in range(4)),
        (coupling_hbm, coupling),
        (modes_hbm, modes),
        (coef_hbm, coef),
        (mass_hbm, mass),
        (kinv_top_hbm, kinv_turned),
        (kinv_low_hbm, kinv_low),
    ]
    fetch = [pltpu.make_async_copy(src, dst, local_sem.at[i]) for i, (src, dst) in enumerate(fetched)]
    for c in fetch:
        c.start()

    @pl.loop(0, 64)
    def _(k):
        found = jnp.int32(0)
        for j in range(24):
            found = jnp.where(anc_low[j] == k, jnp.int32(j + 1), found)
        inv_low[k] = found

    @pl.loop(0, 16)
    def _(k):
        found = jnp.int32(0)
        for j in range(8):
            found = jnp.where(anc_top[j] == k, jnp.int32(j + 1), found)
        inv_top[k] = found

    loads[0] = jnp.zeros(loads.shape[1:], BF16)
    for c in range(2):
        top_loads[c, 0] = jnp.zeros(top_loads.shape[2:], F32)
    for i in range(8):
        fetch[i].wait()
    pl.semaphore_wait(barrier, len(peers))

    comm = Comm(send_sem, recv_sem)
    ga = [gather_steps(comm, low_a[c], low_a[c].at[x, y, z], *lines[0]) for c in range(2)]
    gb = [gather_steps(comm, low_b[c], low_b[c].at[y, x, z], *lines[1]) for c in range(2)]
    gt = top_steps(
        comm, tops, group, mate, across, mate_across, x, y, z, xdev, ydev, zdev, mate_dev, across_dev
    )

    def turn(i):
        @pl.loop(0, 8)
        def _(k):
            cols = pl.ds(pl.multiple_of(k * 256, 256), 256)
            turned[cols, pl.ds(i * 256, 256)] = coupling[pl.ds(i * 256, 256), cols].T

    def turn_modes():
        for i in range(6):
            turned[pl.ds(2048, 128), pl.ds(i * 256, 256)] = modes[pl.ds(i * 256, 256), :].T
        kinv_top[...] = kinv_turned[...].T

    def compute_steps(c):
        cols = pl.ds(c * 256, 256)
        for j in range(8):
            b = anc_top[j]
            for h in range(2):
                for k in range(2):
                    part = tops[b // 4, b % 4, h, 2 * c + k]
                    stacked[pl.ds(j * 64 + h * 32, 32), pl.ds(128 * k, 128)] = part
        for j in range(24):
            k = anc_low[j]
            ky, kz, kx = k // 16, (k // 4) % 4, k % 4
            stacked[pl.ds(512 + j * 64, 32), :] = low_a[c][kx, ky, kz]
            stacked[pl.ds(512 + j * 64 + 32, 32), :] = low_b[c][ky, kx, kz]
        yield
        halves = (pl.ds(0, 768), pl.ds(768, 768))
        got = [jnp.dot(coupling[rows, :], stacked[...], preferred_element_type=F32) for rows in halves]
        more = [jnp.dot(modes[rows, :], coef[:, cols], preferred_element_type=F32) for rows in halves]
        for rows, g, m in zip(halves, got, more):
            shapes[rows, :] = (m - g).astype(BF16)
        yield
        got = [jnp.dot(mass[rows, :], shapes[...], preferred_element_type=F32) for rows in halves]
        for rows, g in zip(halves, got):
            weighted[rows, :] = g.astype(BF16)
        yield
        got = [jnp.dot(turned[pl.ds(256 * i, 256), :], weighted[...], preferred_element_type=F32) for i in range(2)]
        for b in range(8):
            for r in range(8):
                for t in range(2):
                    first = (b % 4) * 64 + r * 8
                    top_loads[c, 1 + b, r, t] = got[b // 4][first : first + 8, t * 128 : t * 128 + 128]

        @pl.loop(0, 64, unroll=4)
        def _(t):
            i, r, k = t // 16, (t // 2) % 8, t % 2
            one = top_loads[c, inv_top[4 * (1 - core) + i], r, k]
            two = top_loads[c, inv_top[8 + 4 * (1 - core) + i], r, k]
            give[c, t] = jnp.concatenate([one, two], axis=0).astype(BF16)

        comm.send(m_swap[c], give.at[c], take.at[c], mate_dev)
        yield
        got = [jnp.dot(turned[pl.ds(512 + 768 * i, 768), :], weighted[...], preferred_element_type=F32) for i in range(2)]
        for b in range(24):
            for h in range(2):
                for r in range(2):
                    for t in range(2):
                        first = (b % 12) * 64 + h * 32 + r * 16
                        part = got[b // 12][first : first + 16, t * 128 : t * 128 + 128]
                        loads[1 + b, h, r * 2 + t] = part.astype(BF16)
        yield

        @pl.loop(0, 64, unroll=4)
        def _(k):
            ky, kz, kx = k // 16, (k // 4) % 4, k % 4
            j = inv_low[k]
            s_low[c, 0, kx, ky, kz] = loads[j, 0]
            s_low[c, 1, ky, kx, kz] = loads[j, 1]

    def project(c):
        cols = pl.ds(c * 256, 256)
        proj[:, cols] = jnp.dot(turned[pl.ds(2048, 128), :], weighted[...], preferred_element_type=F32).astype(BF16)

    def top_path(c):
        q, p = lines[c][:2]
        m, m_line, m_back = comm.ids(15), comm.ids(7), comm.ids(15)
        s, pt, out, got, g = s_top.at[c], tp.at[c], line_out.at[c], line_in.at[c], gath.at[c]
        offsets = [(dq, dp) for dq in range(4) for dp in range(4) if dq + dp > 0]
        plane = sorted(offsets, key=lambda v: -(min(v[0], 4 - v[0]) + min(v[1], 4 - v[1])))

        def plane_dev(v, w):
            return {"leaf": w * 16 + z * 4 + v} if c == 0 else {"leaf": v * 16 + z * 4 + w}

        comm.recv(m_swap[c], take.at[c], mate_dev)

        @pl.loop(0, 64, unroll=4)
        def _(t):
            i, r, k = t // 16, (t // 2) % 8, t % 2
            one = top_loads[c, inv_top[4 * core + i], r, k]
            two = top_loads[c, inv_top[8 + 4 * core + i], r, k]
            mine = jnp.concatenate([one, two], axis=0) + take[c, t].astype(F32)
            s_top[c, t // 16, (t // 4) % 4, t % 4] = mine.astype(BF16)

        for i, (dq, dp) in enumerate(plane):
            to_q, to_p = (q + dq) % 4, (p + dp) % 4
            comm.send(m[i], s.at[to_q, to_p], pt.at[i], plane_dev(to_q, to_p))
        yield
        total = s_top[c, q, p].astype(F32)
        for i, (dq, dp) in enumerate(plane):
            comm.recv(m[i], pt.at[i], plane_dev((q + dq) % 4, (p + dp) % 4))
            total = total + tp[c, i].astype(F32)
        for h in range(2):
            for k in range(2):
                two = [total[2 * k + i, 8 * h : 8 * h + 8] for i in range(2)]
                line_out[c, h, k] = jnp.concatenate(two, axis=0).astype(BF16)
        for d in (1, 2, 3):
            comm.send(m_line[d - 1], out.at[half], got.at[d - 1], zdev((z + d) % 4))
        for d in range(4):
            comm.send(m_line[3 + d], out.at[1 - half], got.at[3 + d], far_zdev((z + d) % 4))
        yield
        total = line_out[c, half].astype(F32)
        for d in (1, 2, 3):
            comm.recv(m_line[d - 1], got.at[d - 1], zdev((z + d) % 4))
            total = total + line_in[c, d - 1].astype(F32)
        for d in range(4):
            comm.recv(m_line[3 + d], got.at[3 + d], far_zdev((z + d) % 4))
            total = total + line_in[c, 3 + d].astype(F32)
        gath[c, q, p] = total.astype(BF16)
        for i, (dq, dp) in enumerate(plane):
            comm.send(m_back[i], g.at[q, p], g.at[q, p], plane_dev((q + dq) % 4, (p + dp) % 4))
        yield
        for i, (dq, dp) in enumerate(plane):
            comm.recv(m_back[i], g.at[(q + 4 - dq) % 4, (p + 4 - dp) % 4], plane_dev((q + dq) % 4, (p + dp) % 4))
        for t in range(64):
            i, r, k = t // 16, (t // 2) % 8, t % 2
            part = gath[c, t // 16, (t // 4) % 4, (t % 4) // 2].astype(F32)[(t % 2) * 8 : (t % 2) * 8 + 8]
            full_top[i, pl.ds(r * 8, 8), pl.ds(c * 256 + k * 128, 128)] = part

    def scatter(c, h):
        return scatter_steps(
            comm, s_low.at[c, h], r1.at[c, h], r2.at[c, h], rp1.at[c, h], rp2.at[c, h], rz.at[c, h], sums.at[c, h],
            *lines[h],
        )

    m_swap = comm.ids(2)

    work = [compute_steps(0), compute_steps(1)]
    sc = [scatter(0, 0), scatter(0, 1), scatter(1, 0), scatter(1, 1)]
    path = [top_path(0), top_path(1)]

    def run_plan(plan):
        for step in plan:
            if step == "a":
                advance(ga[0], gb[0])
            elif step == "b":
                advance(ga[1], gb[1])
            elif step == "t":
                advance(gt)
            elif step in "vw":
                advance(work["vw".index(step)])
            elif step == "s":
                advance(sc[0], sc[1])
            elif step == "u":
                advance(sc[2], sc[3])
            elif step in "pq":
                advance(path["pq".index(step)])
            elif step in "jk":
                project("jk".index(step))
            elif step == "f":
                fetch[8].wait()
            elif step == "6":
                for i in range(9, len(fetch)):
                    fetch[i].wait()
                turn_modes()
            else:
                turn(int(step))

    run_plan(GATHER_PLAN)
    run_together(ga[0], gb[0], gt)
    run_plan(FIRST_PLAN)
    run_together(work[0], ga[1], gb[1])
    run_plan(SECOND_PLAN)
    run_together(work[1])
    run_plan(LAST_PLAN)
    run_together(path[1], sc[0], sc[1], sc[2], sc[3], path[0])

    for c in range(2):
        for h in range(2):
            for r in range(2):
                for t in range(2):
                    rows, cols = pl.ds(h * 32 + r * 16, 16), pl.ds(c * 256 + t * 128, 128)
                    full_low[rows, cols] = sums[c, h, r * 2 + t]
    new_low[...] = jnp.dot(kinv_low[...], full_low[...], preferred_element_type=F32, precision=lax.Precision.HIGHEST)
    for b in range(4):
        rows = pl.ds(b * 64, 64)
        new_top[rows, :] = jnp.dot(
            kinv_top[rows, :], full_top[b], preferred_element_type=F32, precision=lax.Precision.HIGHEST
        )
    comm.finish()


def per_device(top_modes, low_modes, anc_top, anc_low, coupling, leaf_mass, leaf_modes, leaf_coef, kinv_top, kinv_low):
    smem = pl.BlockSpec(memory_space=pltpu.SMEM)
    vmem = pl.BlockSpec(memory_space=pltpu.VMEM)
    hbm = pl.BlockSpec(memory_space=pl.ANY)
    tile, four = (16, 128), (4, 16, 128)
    messages = 4 * 23 + 25 + 4 * 23 + 2 * 37 + 2
    return pl.pallas_call(
        kernel,
        out_shape=(
            jax.ShapeDtypeStruct((256, 512), F32),
            jax.ShapeDtypeStruct((64, 512), F32),
            jax.ShapeDtypeStruct((128, 512), BF16),
        ),
        in_specs=[smem] * 2 + [hbm] * 8,
        out_specs=(vmem, vmem, vmem),
        scratch_shapes=[
            pltpu.VMEM((128, 512), BF16),
            pltpu.VMEM((256, 64), F32),
            pltpu.VMEM((64, 64), F32),
            pltpu.VMEM((1536, 2048), BF16),
            pltpu.VMEM((1536, 1536), BF16),
            pltpu.VMEM((1536, 128), BF16),
            pltpu.VMEM((2176, 1536), BF16),
            pltpu.VMEM((64, 256), F32),
            *([pltpu.VMEM((4, 4, 4, 32, 256), BF16)] * 4),
            pltpu.VMEM((4, 4, 2, 4, 32, 128), BF16),
            pltpu.VMEM((2048, 256), BF16),
            pltpu.VMEM((1536, 256), BF16),
            pltpu.VMEM((1536, 256), BF16),
            pltpu.VMEM((25, 2) + four, BF16),
            pltpu.VMEM((2, 9, 8, 2, 8, 128), F32),
            pltpu.VMEM((2, 64) + tile, BF16),
            pltpu.VMEM((2, 64) + tile, BF16),
            pltpu.VMEM((2, 2, 4, 4, 4) + four, BF16),
            pltpu.VMEM((2, 2, 2, 4, 2) + four, BF16),
            pltpu.VMEM((2, 2, 2, 4, 4) + four, BF16),
            pltpu.VMEM((2, 2, 2, 2) + four, BF16),
            pltpu.VMEM((2, 2, 2, 4) + four, BF16),
            pltpu.VMEM((2, 2, 3) + four, BF16),
            pltpu.VMEM((2, 2) + four, F32),
            pltpu.VMEM((2, 4, 4, 4) + tile, BF16),
            pltpu.VMEM((2, 15, 4) + tile, BF16),
            pltpu.VMEM((2, 2, 2) + tile, BF16),
            pltpu.VMEM((2, 7, 2) + tile, BF16),
            pltpu.VMEM((2, 4, 4, 2) + tile, BF16),
            pltpu.VMEM((4, 64, 512), F32),
            pltpu.VMEM((64, 512), F32),
            pltpu.SMEM((16,), jnp.int32),
            pltpu.SMEM((64,), jnp.int32),
            pltpu.SemaphoreType.DMA((14,)),
            pltpu.SemaphoreType.DMA((messages,)),
            pltpu.SemaphoreType.DMA((messages,)),
        ],
        compiler_params=pltpu.CompilerParams(
            collective_id=0, has_side_effects=True, vmem_limit_bytes=63000 * 1024
        ),
    )(
        anc_top[0], anc_low[0],
        top_modes.reshape(4, 2, 32, 512), low_modes.reshape(2, 32, 512), leaf_coef, kinv_top.T, kinv_low,
        coupling, leaf_mass, leaf_modes,
    )


def solution(mesh):
    both = P(("group", "leaf"), None)
    return jax.shard_map(
        per_device,
        mesh=mesh,
        in_specs=(P("group", None), both, both, both, both, both, both, both, P("group", None), both),
        out_specs=(P("group", None), both, both),
        check_vma=False,
    )
```

time: 129 us -> 97.7 us (0.76)
  Pallas kernels: 119 us -> 91.9 us
  other arithmetic: 2.51 us -> 0 us
  local copies, waits for them, and re-layouts: 6.6 us -> 5 us
    pallas_call x1, Pallas kernels: 119 us -> 91.9 us  [per_device(): pl.pallas_call(kernel, out_shape=(jax.ShapeDtypeStruct((256, 512), F32),...]
    reduce_sum x2 -> x0, other arithmetic: 2.5 us -> none  [the longest x1 1.25 us: per_device(): jnp.sum(jnp.where(anc_low == jnp.arange(64, dtype=jnp.int32)[:, None], jn...]
    unnamed x4 -> x3, local copies, waits for them, and re-layouts: 6.6 us -> 5 us
where the time goes in v2:
time: 97.7 us; the launch traced here: 97.5 us
  Pallas kernels  91.9 us (94%)
  local copies, waits for them, and re-layouts  5 us (5%)
    pallas_call x1, Pallas kernels, per_device(): pl.pallas_call(kernel, out_shape=(jax.ShapeDtypeStruct((256, 512), F32),...  91.9 us
    unnamed x3, local copies, waits for them, and re-layouts  5 us

profile of v2, /device:TPU:6, one launch (start us, length us, event | category | flops | bytes accessed | tf_op | source)
XLA Modules:
  0.0 97.5 jit_solution(6231105445711283976)
XLA Ops:
  0.6 91.9 %shard_map.121 = (f32[256,512]{1,0:T(8,128)}, f32[64,512]{1,0:T(8,128)}, bf16[128,512]{1,0:T(8,128)(2,1)}) custom-call(s32[8]{0:T(128)} %bitcast.8, s32[24]{0:T(128)} %bitcast.9, bf16[4,2,32,512]{3,2,1,0:T(8,128)(2,1)} %bitcast.5, bf16[2,32,512]{2,1,0:T(8,128)(2,1)} %bitcast.6, bf16[128,512]{1,0:T(8,128)(2,1)} %coef_hbm.1, f32[64,256]{1,0:T(8,128)} %bitcast.7, ...), custom_call_target="tpu_custom_call" | custom-call | tf_op jit(solution)/shard_map/pallas_call | solution.py:511
  92.5 1.9 %copy.16 = f32[256,512]{1,0:T(8,128)} copy(f32[256,512]{1,0:T(8,128)} %get-tuple-element.6) | data formatting | bytes 1048576
  94.4 1.6 %copy.17 = f32[64,512]{1,0:T(8,128)} copy(f32[64,512]{1,0:T(8,128)} %get-tuple-element.7) | data formatting | bytes 262144
  95.9 1.6 %copy.18 = bf16[128,512]{1,0:T(8,128)(2,1)} copy(bf16[128,512]{1,0:T(8,128)(2,1)} %get-tuple-element.8) | data formatting | bytes 262144

commit v3 on v2

--- a/solution.py
+++ b/solution.py
@@ -226,13 +226,13 @@
 
 def kernel(
     anc_top, anc_low,
-    top_hbm, low_hbm, coef_hbm, kinv_top_hbm, kinv_low_hbm, coupling_hbm, mass_hbm, modes_hbm,
-    new_top, new_low, proj,
-    coef, kinv_top, kinv_low, coupling, mass, modes, turned, kinv_turned,
+    top_hbm, low_hbm, coef_hbm, coupling_hbm, mass_hbm, modes_hbm,
+    full_top, full_low, proj,
+    coef, coupling, mass, modes, turned,
     low_a0, low_a1, low_b0, low_b1, tops, stacked, shapes, weighted,
     loads, top_loads, give, take,
     s_low, r1, r2, rp1, rp2, rz, sums,
-    s_top, tp, line_out, line_in, gath, full_top, full_low,
+    s_top, tp, line_out, line_in, gath,
     inv_top, inv_low, local_sem, send_sem, recv_sem,
 ):
     low_a, low_b = (low_a0, low_a1), (low_b0, low_b1)
@@ -277,8 +277,6 @@
         (modes_hbm, modes),
         (coef_hbm, coef),
         (mass_hbm, mass),
-        (kinv_top_hbm, kinv_turned),
-        (kinv_low_hbm, kinv_low),
     ]
     fetch = [pltpu.make_async_copy(src, dst, local_sem.at[i]) for i, (src, dst) in enumerate(fetched)]
     for c in fetch:
@@ -321,7 +319,6 @@
     def turn_modes():
         for i in range(6):
             turned[pl.ds(2048, 128), pl.ds(i * 256, 256)] = modes[pl.ds(i * 256, 256), :].T
-        kinv_top[...] = kinv_turned[...].T
 
     def compute_steps(c):
         cols = pl.ds(c * 256, 256)
@@ -493,13 +490,18 @@
                 for t in range(2):
                     rows, cols = pl.ds(h * 32 + r * 16, 16), pl.ds(c * 256 + t * 128, 128)
                     full_low[rows, cols] = sums[c, h, r * 2 + t]
+    comm.finish()
+
+
+def finish_kernel(full_top, full_low, part, kinv_turned, kinv_low, new_top, new_low, proj):
+    proj[...] = part[...]
     new_low[...] = jnp.dot(kinv_low[...], full_low[...], preferred_element_type=F32, precision=lax.Precision.HIGHEST)
+    kinv_top = kinv_turned[...].T
     for b in range(4):
         rows = pl.ds(b * 64, 64)
         new_top[rows, :] = jnp.dot(
-            kinv_top[rows, :], full_top[b], preferred_element_type=F32, precision=lax.Precision.HIGHEST
+            kinv_top[b * 64 : b * 64 + 64], full_top[b], preferred_element_type=F32, precision=lax.Precision.HIGHEST
         )
-    comm.finish()
 
 
 def per_device(top_modes, low_modes, anc_top, anc_low, coupling, leaf_mass, leaf_modes, leaf_coef, kinv_top, kinv_low):
@@ -508,24 +510,21 @@
     hbm = pl.BlockSpec(memory_space=pl.ANY)
     tile, four = (16, 128), (4, 16, 128)
     messages = 4 * 23 + 25 + 4 * 23 + 2 * 37 + 2
-    return pl.pallas_call(
+    full_top, full_low, part = pl.pallas_call(
         kernel,
         out_shape=(
-            jax.ShapeDtypeStruct((256, 512), F32),
+            jax.ShapeDtypeStruct((4, 64, 512), F32),
             jax.ShapeDtypeStruct((64, 512), F32),
             jax.ShapeDtypeStruct((128, 512), BF16),
         ),
-        in_specs=[smem] * 2 + [hbm] * 8,
+        in_specs=[smem] * 2 + [hbm] * 6,
         out_specs=(vmem, vmem, vmem),
         scratch_shapes=[
             pltpu.VMEM((128, 512), BF16),
-            pltpu.VMEM((256, 64), F32),
-            pltpu.VMEM((64, 64), F32),
             pltpu.VMEM((1536, 2048), BF16),
             pltpu.VMEM((1536, 1536), BF16),
             pltpu.VMEM((1536, 128), BF16),
             pltpu.VMEM((2176, 1536), BF16),
-            pltpu.VMEM((64, 256), F32),
             *([pltpu.VMEM((4, 4, 4, 32, 256), BF16)] * 4),
             pltpu.VMEM((4, 4, 2, 4, 32, 128), BF16),
             pltpu.VMEM((2048, 256), BF16),
@@ -547,11 +546,9 @@
             pltpu.VMEM((2, 2, 2) + tile, BF16),
             pltpu.VMEM((2, 7, 2) + tile, BF16),
             pltpu.VMEM((2, 4, 4, 2) + tile, BF16),
-            pltpu.VMEM((4, 64, 512), F32),
-            pltpu.VMEM((64, 512), F32),
             pltpu.SMEM((16,), jnp.int32),
             pltpu.SMEM((64,), jnp.int32),
-            pltpu.SemaphoreType.DMA((14,)),
+            pltpu.SemaphoreType.DMA((12,)),
             pltpu.SemaphoreType.DMA((messages,)),
             pltpu.SemaphoreType.DMA((messages,)),
         ],
@@ -560,9 +557,19 @@
         ),
     )(
         anc_top[0], anc_low[0],
-        top_modes.reshape(4, 2, 32, 512), low_modes.reshape(2, 32, 512), leaf_coef, kinv_top.T, kinv_low,
+        top_modes.reshape(4, 2, 32, 512), low_modes.reshape(2, 32, 512), leaf_coef,
         coupling, leaf_mass, leaf_modes,
     )
+    return pl.pallas_call(
+        finish_kernel,
+        out_shape=(
+            jax.ShapeDtypeStruct((256, 512), F32),
+            jax.ShapeDtypeStruct((64, 512), F32),
+            jax.ShapeDtypeStruct((128, 512), BF16),
+        ),
+        in_specs=[vmem] * 5,
+        out_specs=(vmem, vmem, vmem),
+    )(full_top, full_low, part, kinv_top.T, kinv_low)
 
 
 def solution(mesh):

time: 97.7 us -> 94.5 us (0.967)
  local copies, waits for them, and re-layouts: 5 us -> 0 us
  Pallas kernels: 91.9 us -> 93.8 us
    unnamed x3 -> x0, local copies, waits for them, and re-layouts: 5 us -> none
    pallas_call x1 -> x2, Pallas kernels: 91.9 us -> 93.8 us  [the longest x1 91.1 us: per_device(): pl.pallas_call(kernel, out_shape=(jax.ShapeDtypeStruct((4, 64, 512), F32)...]
where the time goes in v3:
time: 94.5 us; the launch traced here: 94.4 us
  Pallas kernels  93.8 us (99%)
    pallas_call x1, Pallas kernels, per_device(): pl.pallas_call(kernel, out_shape=(jax.ShapeDtypeStruct((4, 64, 512), F32)...  91.1 us
    pallas_call x1, Pallas kernels, per_device(): pl.pallas_call(finish_kernel, out_shape=(jax.ShapeDtypeStruct((256, 512),...  2.63 us

profile of v3, /device:TPU:6, one launch (start us, length us, event | category | flops | bytes accessed | tf_op | source)
XLA Modules:
  0.0 94.4 jit_solution(13576468612971596384)
XLA Ops:
  0.6 91.1 %shard_map.121 = (f32[4,64,512]{2,1,0:T(8,128)}, f32[64,512]{1,0:T(8,128)}, bf16[128,512]{1,0:T(8,128)(2,1)}) custom-call(s32[8]{0:T(128)} %bitcast.8, s32[24]{0:T(128)} %bitcast.9, bf16[4,2,32,512]{3,2,1,0:T(8,128)(2,1)} %bitcast.5, bf16[2,32,512]{2,1,0:T(8,128)(2,1)} %bitcast.6, bf16[128,512]{1,0:T(8,128)(2,1)} %coef_hbm.1, ...), custom_call_target="tpu_custom_call" | custom-call | tf_op jit(solution)/shard_map/pallas_call | solution.py:513
  91.8 2.6 %shard_map.122 = (f32[256,512]{1,0:T(8,128)}, f32[64,512]{1,0:T(8,128)}, bf16[128,512]{1,0:T(8,128)(2,1)}) custom-call(f32[4,64,512]{2,1,0:T(8,128)} %get-tuple-element.6.full_top, f32[64,512]{1,0:T(8,128)} %get-tuple-element.7.full_low, bf16[128,512]{1,0:T(8,128)(2,1)} %get-tuple-element.8.part, f32[64,256]{1,0:T(8,128)} %bitcast.7, f32[64,64]{1,0:T(8,128)} %kinv_low.1), custom_call_target="tpu_custom_call" | custom-call | tf_op jit(solution)/shard_map/pallas_call | solution.py:563
